TPU v7x, 512 devices: a whole 4x4x16 slice. The times are simulated.
512 devices in a mesh: blk: 64 (over z, x_lo, core), rep: 8 (over y, x_hi).
Axes of the slice: x: 4 (x_hi: 2, x_lo: 2; x = x_hi * 2 + x_lo), y: 4, z: 16, core: 2. Of those that a mesh axis runs over, the one named last changes fastest.
Arguments:
- features: bfloat16 [65536, 256], P(('blk', 'rep')), may hold values from -6 to 6
- out_grad: bfloat16 [65536, 256], P('blk'), may hold values from -4 to 4
- weight: bfloat16 [256, 256], replicated, may hold values from -0.375 to 0.375
- block_words: int32 [64, 64, 8, 16, 128], P('blk', 'rep'), may hold values from 0 to 255
- block_coords: int32 [64, 64, 2, 8], P('blk', 'rep'), may hold values from 0 to 7, as said below
- block_counts: int32 [64, 64], P('blk', 'rep'), may hold values from 1 to 8, as said below
- degrees: int32 [65536], P('blk'), may hold values from 1 to 127
Outputs:
- input_grad: bfloat16 [65536, 256], P(('blk', 'rep'))
- weight_grad: float32 [256, 256], replicated
Inputs may be any that keep to these rules, and one draw needn't show every extreme that they name: `block_coords`: within one slab pair the 8 slots name distinct pairs of row block and column block. `block_counts`: the 8 slab pairs of one device include one in which all 8 slots are live.
All inputs are finite; a program needn't handle non-finite values.
Results may differ from a plain program's by a relative error of at most 0.015.
Values may be sent and summed in bfloat16 or wider, within the bound.
A program may use at most 64 MiB of HBM per device.

v0:
```python
import math
import jax
import jax.numpy as jnp
from jax import lax
from jax.sharding import PartitionSpec as P


def from_behind(block, axis, distance):
    devices = range(lax.axis_size(axis))
    route = [((i - distance) % len(devices), i) for i in devices]
    return lax.ppermute(block, axis, route)


def unpack_block(slot_words):
    shifts = jnp.arange(8, dtype=jnp.int32)
    bit_values = jnp.bitwise_and(
        jnp.right_shift(slot_words[:, :, None, :], shifts[None, None, :, None]), 1
    )
    return bit_values.reshape(slot_words.shape[0], 128, 128).astype(jnp.bfloat16)


def per_device(features, out_grad, weight, block_words, block_coords, block_counts, degrees):
    slab_rows, width = out_grad.shape
    row_blocks = slab_rows // 128
    group_size = lax.axis_size("rep")
    step_count = lax.axis_size("blk") // group_size
    rep_index = lax.axis_index("rep")
    inverse_root = lax.rsqrt(degrees.astype(jnp.float32))
    scaled = (out_grad.astype(jnp.float32) * inverse_root[:, None]).astype(jnp.bfloat16)
    column_ids = jnp.arange(row_blocks, dtype=jnp.int32)
    slot_total = block_words.shape[2]
    slot_ids = jnp.arange(slot_total, dtype=jnp.int32)

    def add_slot(accumulated, source_slab, slot_index):
        slot_words = lax.dynamic_index_in_dim(block_words[0], slot_index, 0, keepdims=False)
        coords = lax.dynamic_index_in_dim(block_coords[0], slot_index, 0, keepdims=False)
        live_count = lax.dynamic_index_in_dim(block_counts[0], slot_index, 0, keepdims=False)
        picked = jnp.take(source_slab.reshape(row_blocks, 128, width), coords[0], axis=0)
        transposed = unpack_block(slot_words)
        contrib = jnp.einsum("bvu,buf->bvf", transposed, picked, preferred_element_type=jnp.float32)
        live_slots = slot_ids < live_count
        placement = ((coords[1][:, None] == column_ids[None, :]) & live_slots[:, None]).astype(
            jnp.float32
        )
        return accumulated + jnp.einsum("bc,bvf->cvf", placement, contrib)

    empty = jnp.zeros((row_blocks, 128, width), jnp.float32)
    current = scaled
    for bit in range(group_size.bit_length() - 1):
        shifted = from_behind(current, "blk", -(1 << bit) * step_count)
        current = jnp.where(
            jnp.bitwise_and(jnp.right_shift(rep_index, bit), 1) == 1, shifted, current
        )
    accumulated = add_slot(empty, current, 0)

    def advance(step_index, state_tuple):
        current, accumulated = state_tuple
        current = from_behind(current, "blk", -1)
        return (current, add_slot(accumulated, current, step_index))

    current, accumulated = lax.fori_loop(1, step_count, advance, (current, accumulated))
    partial_sums = accumulated.reshape(slab_rows, width)
    share_rows = slab_rows // group_size
    share_root = lax.dynamic_slice_in_dim(inverse_root, rep_index * share_rows, share_rows, 0)
    whole_sums = lax.psum(partial_sums, "rep")
    own_sums = lax.dynamic_slice_in_dim(whole_sums, rep_index * share_rows, share_rows, 0)
    aggregated = (own_sums * share_root[:, None]).astype(jnp.bfloat16)
    input_grad = lax.dot_general(
        aggregated, weight, (((1,), (1,)), ((), ())), preferred_element_type=jnp.float32
    ).astype(jnp.bfloat16)
    weight_term = lax.dot_general(
        features, aggregated, (((0,), (0,)), ((), ())), preferred_element_type=jnp.float32
    )
    node_total = slab_rows * lax.axis_size("blk")
    weight_grad = lax.psum(weight_term, ("blk", "rep")) * (1.0 / math.sqrt(node_total))
    return (input_grad, weight_grad)


def solution(mesh):
    return jax.shard_map(
        per_device,
        mesh=mesh,
        in_specs=(
            P(("blk", "rep"), None),
            P("blk", None),
            P(),
            P("blk", "rep", None, None, None),
            P("blk", "rep", None, None),
            P("blk", "rep"),
            P("blk"),
        ),
        out_specs=(P(("blk", "rep"), None), P()),
        check_vma=False,
    )
```

profile of v0, /device:TPU:4, one launch (start us, length us, event | category | flops | bytes accessed | tf_op | source)
XLA Modules:
  0.0 821.2 jit_solution(11861567313591803345)
XLA Ops:
  9.3 11.8 %collective-permute-start.1 = (bf16[1024,256]{1,0:T(8,128)(2,1)S(1)}, bf16[1024,256]{1,0:T(8,128)(2,1)S(1)}, u32[]{:S(2)}, u32[]{:S(2)}) collective-permute-start(bf16[1024,256]{1,0:T(8,128)(2,1)S(1)} %multiply_convert_fusion), channel_id=1, source_target_pairs={{64,0},{72,8},{80,16},{88,24},{96,32},{104,40},{112,48},{120,56},{... | collective-permute-start | bytes 1572872 | tf_op jit(solution)/shard_map/ppermute | solution.py:11
  21.1 22.4 %collective-permute-done.1 = bf16[1024,256]{1,0:T(8,128)(2,1)S(1)} collective-permute-done((bf16[1024,256]{1,0:T(8,128)(2,1)S(1)}, bf16[1024,256]{1,0:T(8,128)(2,1)S(1)}, u32[]{:S(2)}, u32[]{:S(2)}) %collective-permute-start.1) | collective-permute-done | bytes 524320 | tf_op jit(solution)/shard_map/ppermute | solution.py:11
  43.8 6.3 collective-permute-start.2
  51.0 40.0 %collective-permute-done.2 = bf16[1024,256]{1,0:T(8,128)(2,1)S(1)} collective-permute-done((bf16[1024,256]{1,0:T(8,128)(2,1)S(1)}, bf16[1024,256]{1,0:T(8,128)(2,1)S(1)}, u32[]{:S(2)}, u32[]{:S(2)}) %collective-permute-start.2) | collective-permute-done | bytes 524320 | tf_op jit(solution)/shard_map/ppermute | solution.py:11
  91.1 5.0 collective-permute-start.3
  98.3 28.4 %collective-permute-done.3 = bf16[1024,256]{1,0:T(8,128)(2,1)S(1)} collective-permute-done((bf16[1024,256]{1,0:T(8,128)(2,1)S(1)}, bf16[1024,256]{1,0:T(8,128)(2,1)S(1)}, u32[]{:S(2)}, u32[]{:S(2)}) %collective-permute-start.3) | collective-permute-done | bytes 524320 | tf_op jit(solution)/shard_map/ppermute | solution.py:11
  128.1 121.5 %while.20 = (s32[]{:T(128)}, bf16[1024,256]{1,0:T(8,128)(2,1)S(1)}, f32[8,128,256]{2,0,1:T(8,128)S(1)}, s32[1,8,2,8]{3,2,1,0:T(2,128)}, s32[1,8]{1,0:T(1,128)S(1...) while((s32[]{:T(128)}, bf16[1024,256]{1,0:T(8,128)(2,1)S(1)}, ...), condition=%wide.region_1.3_spmd.clone.clone, body=%wide.region_0.2_spmd.clone.clone.sunk | while | flops 72221880 | bytes 8067647 | solution.py:61
  128.2 29.0 %collective-permute-start = (bf16[1024,256]{1,0:T(8,128)(2,1)S(1)}, bf16[1024,256]{1,0:T(8,128)(2,1)S(1)}, u32[]{:S(2)}, u32[]{:S(2)}) collective-permute-start(bf16[1024,256]{1,0:T(8,128)(2,1)S(1)} %get-tuple-element.308), channel_id=1, source_target_pairs={{8,0},{16,8},{24,16},{32,24},{40,32},{48,40},{56,48},{64,56},{72,6... | collective-permute-start | bytes 1572872 | tf_op jit(solution)/shard_map/while/body/eval_jaxpr/ppermute | solution.py:11
  160.1 3.8 collective-permute-done
  165.3 5.9 collective-permute-start
  174.2 3.8 collective-permute-done
  179.4 5.9 collective-permute-start
  188.2 3.8 collective-permute-done
  193.4 5.9 collective-permute-start
  202.3 3.8 collective-permute-done
  207.5 5.9 collective-permute-start
  216.3 3.8 collective-permute-done
  221.6 5.9 collective-permute-start
  230.4 3.8 collective-permute-done
  235.6 5.9 collective-permute-start
  244.5 3.8 collective-permute-done
  251.2 97.1 %all-reduce.3.cloned.1.call-done = f32[1024,256]{1,0:T(8,128)} async-done(((f32[1024,256]{1,0:T(8,128)}), f32[1024,256]{1,0:T(8,128)}) %all-reduce.3.cloned.1.call-update) | async-done | bytes 1048592 | tf_op jit(solution)/shard_map/psum | solution.py:65
  348.3 1.9 convolution_bitcast_fusion
  352.0 460.6 %all-reduce.5.cloned.1.call-done = f32[256,256]{0,1:T(8,128)} async-done(((f32[256,256]{0,1:T(8,128)}), f32[256,256]{0,1:T(8,128)}) %all-reduce.5.cloned.1.call-update) | async-done | bytes 262160 | tf_op jit(solution)/shard_map/psum | solution.py:75
  (123 shorter events, 41.9 us)
Async XLA Ops:
  7.2 343.1 %copy-start = (bf16[256,256]{1,0:T(8,128)(2,1)S(1)}, bf16[256,256]{1,0:T(8,128)(2,1)}, u32[]{:S(2)}) copy-start(bf16[256,256]{1,0:T(8,128)(2,1)} %param.13) | copy-start | bytes 393220
  7.2 341.1 %all-reduce.3.cloned.1.call-start = ((), (), s32[]{:S(2)}) async-start(), calls=%async_computation | async-start | bytes 2097152 | tf_op jit(solution)/shard_map/psum | solution.py:65
  7.9 35.6 %copy-start.1 = (bf16[1024,256]{1,0:T(8,128)(2,1)S(1)}, bf16[1024,256]{1,0:T(8,128)(2,1)}, u32[]{:S(2)}) copy-start(bf16[1024,256]{1,0:T(8,128)(2,1)} %param.12) | copy-start | bytes 1572868
  9.3 34.2 %collective-permute-start.1 = (bf16[1024,256]{1,0:T(8,128)(2,1)S(1)}, bf16[1024,256]{1,0:T(8,128)(2,1)S(1)}, u32[]{:S(2)}, u32[]{:S(2)}) collective-permute-start(bf16[1024,256]{1,0:T(8,128)(2,1)S(1)} %multiply_convert_fusion), channel_id=1, source_target_pairs={{64,0},{72,8},{80,16},{88,24},{96,32},{104,40},{112,48},{120,56},{... | collective-permute-start | bytes 1572872 | tf_op jit(solution)/shard_map/ppermute | solution.py:11
  43.8 47.2 %collective-permute-start.2 = (bf16[1024,256]{1,0:T(8,128)(2,1)S(1)}, bf16[1024,256]{1,0:T(8,128)(2,1)S(1)}, u32[]{:S(2)}, u32[]{:S(2)}) collective-permute-start(bf16[1024,256]{1,0:T(8,128)(2,1)S(1)} %broadcast_select_fusion), channel_id=1, source_target_pairs={{128,0},{136,8},{144,16},{152,24},{160,32},{168,40},{176,48},{184,... | collective-permute-start | bytes 1572872 | tf_op jit(solution)/shard_map/ppermute | solution.py:11
  91.1 35.7 %collective-permute-start.3 = (bf16[1024,256]{1,0:T(8,128)(2,1)S(1)}, bf16[1024,256]{1,0:T(8,128)(2,1)S(1)}, u32[]{:S(2)}, u32[]{:S(2)}) collective-permute-start(bf16[1024,256]{1,0:T(8,128)(2,1)S(1)} %broadcast_select_fusion.1), channel_id=1, source_target_pairs={{256,0},{264,8},{272,16},{280,24},{288,32},{296,40},{304,48},{312,... | collective-permute-start | bytes 1572872 | tf_op jit(solution)/shard_map/ppermute | solution.py:11
  96.0 0.7 copy-start.3
  128.2 35.7 %collective-permute-start = (bf16[1024,256]{1,0:T(8,128)(2,1)S(1)}, bf16[1024,256]{1,0:T(8,128)(2,1)S(1)}, u32[]{:S(2)}, u32[]{:S(2)}) collective-permute-start(bf16[1024,256]{1,0:T(8,128)(2,1)S(1)} %get-tuple-element.308), channel_id=1, source_target_pairs={{8,0},{16,8},{24,16},{32,24},{40,32},{48,40},{56,48},{64,56},{72,6... | collective-permute-start | bytes 1572872 | tf_op jit(solution)/shard_map/while/body/eval_jaxpr/ppermute | solution.py:11
  165.3 12.6 %collective-permute-start = (bf16[1024,256]{1,0:T(8,128)(2,1)S(1)}, bf16[1024,256]{1,0:T(8,128)(2,1)S(1)}, u32[]{:S(2)}, u32[]{:S(2)}) collective-permute-start(bf16[1024,256]{1,0:T(8,128)(2,1)S(1)} %get-tuple-element.308), channel_id=1, source_target_pairs={{8,0},{16,8},{24,16},{32,24},{40,32},{48,40},{56,48},{64,56},{72,6... | collective-permute-start | bytes 1572872 | tf_op jit(solution)/shard_map/while/body/eval_jaxpr/ppermute | solution.py:11
  179.4 12.6 %collective-permute-start = (bf16[1024,256]{1,0:T(8,128)(2,1)S(1)}, bf16[1024,256]{1,0:T(8,128)(2,1)S(1)}, u32[]{:S(2)}, u32[]{:S(2)}) collective-permute-start(bf16[1024,256]{1,0:T(8,128)(2,1)S(1)} %get-tuple-element.308), channel_id=1, source_target_pairs={{8,0},{16,8},{24,16},{32,24},{40,32},{48,40},{56,48},{64,56},{72,6... | collective-permute-start | bytes 1572872 | tf_op jit(solution)/shard_map/while/body/eval_jaxpr/ppermute | solution.py:11
  193.4 12.6 %collective-permute-start = (bf16[1024,256]{1,0:T(8,128)(2,1)S(1)}, bf16[1024,256]{1,0:T(8,128)(2,1)S(1)}, u32[]{:S(2)}, u32[]{:S(2)}) collective-permute-start(bf16[1024,256]{1,0:T(8,128)(2,1)S(1)} %get-tuple-element.308), channel_id=1, source_target_pairs={{8,0},{16,8},{24,16},{32,24},{40,32},{48,40},{56,48},{64,56},{72,6... | collective-permute-start | bytes 1572872 | tf_op jit(solution)/shard_map/while/body/eval_jaxpr/ppermute | solution.py:11
  207.5 12.6 %collective-permute-start = (bf16[1024,256]{1,0:T(8,128)(2,1)S(1)}, bf16[1024,256]{1,0:T(8,128)(2,1)S(1)}, u32[]{:S(2)}, u32[]{:S(2)}) collective-permute-start(bf16[1024,256]{1,0:T(8,128)(2,1)S(1)} %get-tuple-element.308), channel_id=1, source_target_pairs={{8,0},{16,8},{24,16},{32,24},{40,32},{48,40},{56,48},{64,56},{72,6... | collective-permute-start | bytes 1572872 | tf_op jit(solution)/shard_map/while/body/eval_jaxpr/ppermute | solution.py:11
  221.6 12.6 %collective-permute-start = (bf16[1024,256]{1,0:T(8,128)(2,1)S(1)}, bf16[1024,256]{1,0:T(8,128)(2,1)S(1)}, u32[]{:S(2)}, u32[]{:S(2)}) collective-permute-start(bf16[1024,256]{1,0:T(8,128)(2,1)S(1)} %get-tuple-element.308), channel_id=1, source_target_pairs={{8,0},{16,8},{24,16},{32,24},{40,32},{48,40},{56,48},{64,56},{72,6... | collective-permute-start | bytes 1572872 | tf_op jit(solution)/shard_map/while/body/eval_jaxpr/ppermute | solution.py:11
  235.6 12.6 %collective-permute-start = (bf16[1024,256]{1,0:T(8,128)(2,1)S(1)}, bf16[1024,256]{1,0:T(8,128)(2,1)S(1)}, u32[]{:S(2)}, u32[]{:S(2)}) collective-permute-start(bf16[1024,256]{1,0:T(8,128)(2,1)S(1)} %get-tuple-element.308), channel_id=1, source_target_pairs={{8,0},{16,8},{24,16},{32,24},{40,32},{48,40},{56,48},{64,56},{72,6... | collective-permute-start | bytes 1572872 | tf_op jit(solution)/shard_map/while/body/eval_jaxpr/ppermute | solution.py:11
  251.0 97.3 %copy-start.2 = (bf16[128,256]{1,0:T(8,128)(2,1)S(1)}, bf16[128,256]{1,0:T(8,128)(2,1)}, u32[]{:S(2)}) copy-start(bf16[128,256]{1,0:T(8,128)(2,1)} %param.11) | copy-start | bytes 196612
  251.0 561.5 %all-reduce.5.cloned.1.call-start = ((), (), s32[]{:S(2)}) async-start(), calls=%async_computation.1 | async-start | bytes 524288 | tf_op jit(solution)/shard_map/psum | solution.py:75
Sparse Core Ops, SparseCore 0:
  251.2 97.1 all-reduce.2
  354.3 458.2 all-reduce.4
where the time goes:
time: 822 us; the launch traced here: 821 us
  waiting for transfers between devices  675 us (82%)
  starting transfers between devices  87.8 us (11%)
  local copies, waits for them, and re-layouts  24.9 us (3%)
  between operations  14.2 us (2%)
  matrix products  9.97 us (1%)
  other arithmetic  8.83 us (1%)
    psum x1, waiting for transfers between devices, per_device(): lax.psum(weight_term, ('blk', 'rep')) * (1.0 / math.sqrt(node_total))  461 us
    ppermute x10, waiting for transfers between devices, from_behind(): return lax.ppermute(block, axis, route)  117 us
    psum x1, waiting for transfers between devices, per_device(): whole_sums = lax.psum(partial_sums, 'rep')  97.1 us
    ppermute x10, starting transfers between devices, from_behind(): return lax.ppermute(block, axis, route)  87.7 us
  transfers between devices with their start and end apart: 12, of which 12 were waited for; matrix products, arithmetic and copies ran while one was open for 3% of the time, Pallas kernels for 0%

commit v1 on v0

--- a/solution.py
+++ b/solution.py
@@ -72,7 +72,7 @@
         features, aggregated, (((0,), (0,)), ((), ())), preferred_element_type=jnp.float32
     )
     node_total = slab_rows * lax.axis_size("blk")
-    weight_grad = lax.psum(weight_term, ("blk", "rep")) * (1.0 / math.sqrt(node_total))
+    weight_grad = lax.psum(lax.psum(weight_term, "blk"), "rep") * (1.0 / math.sqrt(node_total))
     return (input_grad, weight_grad)
 
 

time: 822 us -> 863 us (1.050)
  the two profiles are of different devices: /device:TPU:4 before, /device:TPU:32 now
where the time goes in v1:
time: 863 us; the launch traced here: 862 us
  waiting for transfers between devices  733 us (85%)
  starting transfers between devices  71 us (8%)
  local copies, waits for them, and re-layouts  24.9 us (3%)
  between operations  13.9 us (2%)
  matrix products  9.98 us (1%)
  other arithmetic  8.83 us (1%)
    psum x1, waiting for transfers between devices, per_device(): lax.psum(weight_term, 'blk')  396 us
    psum x1, waiting for transfers between devices, per_device(): whole_sums = lax.psum(partial_sums, 'rep')  121 us
    ppermute x10, waiting for transfers between devices, from_behind(): return lax.ppermute(block, axis, route)  113 us
    psum x1, waiting for transfers between devices, per_device(): lax.psum(lax.psum(weight_term, 'blk'), 'rep')  103 us
    ppermute x10, starting transfers between devices, from_behind(): return lax.ppermute(block, axis, route)  70.8 us
  transfers between devices with their start and end apart: 13, of which 13 were waited for; matrix products, arithmetic and copies ran while one was open for 3% of the time, Pallas kernels for 0%

profile of v1, /device:TPU:32, one launch (start us, length us, event | category | flops | bytes accessed | tf_op | source)
XLA Modules:
  0.0 861.7 jit_solution(14030550864121514246)
XLA Ops:
  9.3 10.9 %collective-permute-start.1 = (bf16[1024,256]{1,0:T(8,128)(2,1)S(1)}, bf16[1024,256]{1,0:T(8,128)(2,1)S(1)}, u32[]{:S(2)}, u32[]{:S(2)}) collective-permute-start(bf16[1024,256]{1,0:T(8,128)(2,1)S(1)} %multiply_convert_fusion), channel_id=1, source_target_pairs={{64,0},{72,8},{80,16},{88,24},{96,32},{104,40},{112,48},{120,56},{... | collective-permute-start | bytes 1572872 | tf_op jit(solution)/shard_map/ppermute | solution.py:11
  20.2 19.1 %collective-permute-done.1 = bf16[1024,256]{1,0:T(8,128)(2,1)S(1)} collective-permute-done((bf16[1024,256]{1,0:T(8,128)(2,1)S(1)}, bf16[1024,256]{1,0:T(8,128)(2,1)S(1)}, u32[]{:S(2)}, u32[]{:S(2)}) %collective-permute-start.1) | collective-permute-done | bytes 524320 | tf_op jit(solution)/shard_map/ppermute | solution.py:11
  39.6 6.8 collective-permute-start.2
  47.2 22.3 %collective-permute-done.2 = bf16[1024,256]{1,0:T(8,128)(2,1)S(1)} collective-permute-done((bf16[1024,256]{1,0:T(8,128)(2,1)S(1)}, bf16[1024,256]{1,0:T(8,128)(2,1)S(1)}, u32[]{:S(2)}, u32[]{:S(2)}) %collective-permute-start.2) | collective-permute-done | bytes 524320 | tf_op jit(solution)/shard_map/ppermute | solution.py:11
  69.6 8.2 collective-permute-start.3
  80.0 38.1 %collective-permute-done.3 = bf16[1024,256]{1,0:T(8,128)(2,1)S(1)} collective-permute-done((bf16[1024,256]{1,0:T(8,128)(2,1)S(1)}, bf16[1024,256]{1,0:T(8,128)(2,1)S(1)}, u32[]{:S(2)}, u32[]{:S(2)}) %collective-permute-start.3) | collective-permute-done | bytes 524320 | tf_op jit(solution)/shard_map/ppermute | solution.py:11
  119.6 108.6 %while.20 = (s32[]{:T(128)}, bf16[1024,256]{1,0:T(8,128)(2,1)S(1)}, f32[8,128,256]{2,0,1:T(8,128)S(1)}, s32[1,8,2,8]{3,2,1,0:T(2,128)}, s32[1,8]{1,0:T(1,128)S(1...) while((s32[]{:T(128)}, bf16[1024,256]{1,0:T(8,128)(2,1)S(1)}, ...), condition=%wide.region_1.3_spmd.clone.clone, body=%wide.region_0.2_spmd.clone.clone.sunk | while | flops 72221880 | bytes 8067647 | solution.py:61
  119.6 9.8 %collective-permute-start = (bf16[1024,256]{1,0:T(8,128)(2,1)S(1)}, bf16[1024,256]{1,0:T(8,128)(2,1)S(1)}, u32[]{:S(2)}, u32[]{:S(2)}) collective-permute-start(bf16[1024,256]{1,0:T(8,128)(2,1)S(1)} %get-tuple-element.308), channel_id=1, source_target_pairs={{8,0},{16,8},{24,16},{32,24},{40,32},{48,40},{56,48},{64,56},{72,6... | collective-permute-start | bytes 1572872 | tf_op jit(solution)/shard_map/while/body/eval_jaxpr/ppermute | solution.py:11
  132.3 3.8 collective-permute-done
  137.6 4.7 collective-permute-start
  145.2 9.1 %collective-permute-done = bf16[1024,256]{1,0:T(8,128)(2,1)S(1)} collective-permute-done((bf16[1024,256]{1,0:T(8,128)(2,1)S(1)}, bf16[1024,256]{1,0:T(8,128)(2,1)S(1)}, u32[]{:S(2)}, u32[]{:S(2)}) %collective-permute-start) | collective-permute-done | bytes 524320 | tf_op jit(solution)/shard_map/while/body/eval_jaxpr/ppermute | solution.py:11
  155.7 4.7 collective-permute-start
  163.4 3.8 collective-permute-done
  168.6 4.7 collective-permute-start
  176.2 5.1 collective-permute-done
  182.8 9.2 %collective-permute-start = (bf16[1024,256]{1,0:T(8,128)(2,1)S(1)}, bf16[1024,256]{1,0:T(8,128)(2,1)S(1)}, u32[]{:S(2)}, u32[]{:S(2)}) collective-permute-start(bf16[1024,256]{1,0:T(8,128)(2,1)S(1)} %get-tuple-element.308), channel_id=1, source_target_pairs={{8,0},{16,8},{24,16},{32,24},{40,32},{48,40},{56,48},{64,56},{72,6... | collective-permute-start | bytes 1572872 | tf_op jit(solution)/shard_map/while/body/eval_jaxpr/ppermute | solution.py:11
  194.8 3.8 collective-permute-done
  200.1 5.9 collective-permute-start
  208.9 3.8 collective-permute-done
  214.1 5.9 collective-permute-start
  223.0 3.8 collective-permute-done
  229.7 121.3 %all-reduce.4.cloned.1.call-done = f32[1024,256]{1,0:T(8,128)} async-done(((f32[1024,256]{1,0:T(8,128)}), f32[1024,256]{1,0:T(8,128)}) %all-reduce.4.cloned.1.call-update) | async-done | bytes 1048592 | tf_op jit(solution)/shard_map/psum | solution.py:65
  352.9 396.1 %all-reduce.6.cloned.1.call-done = f32[256,256]{0,1:T(8,128)} async-done(((f32[256,256]{0,1:T(8,128)}), f32[256,256]{0,1:T(8,128)}) %all-reduce.6.cloned.1.call-update) | async-done | bytes 262160 | tf_op jit(solution)/shard_map/psum | solution.py:75
  750.8 102.6 %all-reduce.8.cloned.1.call-done = f32[256,256]{0,1:T(8,128)} async-done(((f32[256,256]{0,1:T(8,128)}), f32[256,256]{0,1:T(8,128)}) %all-reduce.8.cloned.1.call-update) | async-done | bytes 262160 | tf_op jit(solution)/shard_map/psum | solution.py:75
  (126 shorter events, 43.8 us)
Async XLA Ops:
  7.2 741.8 %copy-start = (bf16[256,256]{1,0:T(8,128)(2,1)S(1)}, bf16[256,256]{1,0:T(8,128)(2,1)}, u32[]{:S(2)}) copy-start(bf16[256,256]{1,0:T(8,128)(2,1)} %param.13) | copy-start | bytes 393220
  7.2 343.8 %all-reduce.4.cloned.1.call-start = ((), (), s32[]{:S(2)}) async-start(), calls=%async_computation | async-start | bytes 2097152 | tf_op jit(solution)/shard_map/psum | solution.py:65
  7.9 31.4 %copy-start.1 = (bf16[1024,256]{1,0:T(8,128)(2,1)S(1)}, bf16[1024,256]{1,0:T(8,128)(2,1)}, u32[]{:S(2)}) copy-start(bf16[1024,256]{1,0:T(8,128)(2,1)} %param.12) | copy-start | bytes 1572868
  9.3 30.0 %collective-permute-start.1 = (bf16[1024,256]{1,0:T(8,128)(2,1)S(1)}, bf16[1024,256]{1,0:T(8,128)(2,1)S(1)}, u32[]{:S(2)}, u32[]{:S(2)}) collective-permute-start(bf16[1024,256]{1,0:T(8,128)(2,1)S(1)} %multiply_convert_fusion), channel_id=1, source_target_pairs={{64,0},{72,8},{80,16},{88,24},{96,32},{104,40},{112,48},{120,56},{... | collective-permute-start | bytes 1572872 | tf_op jit(solution)/shard_map/ppermute | solution.py:11
  39.6 29.9 %collective-permute-start.2 = (bf16[1024,256]{1,0:T(8,128)(2,1)S(1)}, bf16[1024,256]{1,0:T(8,128)(2,1)S(1)}, u32[]{:S(2)}, u32[]{:S(2)}) collective-permute-start(bf16[1024,256]{1,0:T(8,128)(2,1)S(1)} %broadcast_select_fusion), channel_id=1, source_target_pairs={{128,0},{136,8},{144,16},{152,24},{160,32},{168,40},{176,48},{184,... | collective-permute-start | bytes 1572872 | tf_op jit(solution)/shard_map/ppermute | solution.py:11
  69.6 48.6 %collective-permute-start.3 = (bf16[1024,256]{1,0:T(8,128)(2,1)S(1)}, bf16[1024,256]{1,0:T(8,128)(2,1)S(1)}, u32[]{:S(2)}, u32[]{:S(2)}) collective-permute-start(bf16[1024,256]{1,0:T(8,128)(2,1)S(1)} %broadcast_select_fusion.1), channel_id=1, source_target_pairs={{256,0},{264,8},{272,16},{280,24},{288,32},{296,40},{304,48},{312,... | collective-permute-start | bytes 1572872 | tf_op jit(solution)/shard_map/ppermute | solution.py:11
  77.8 0.7 copy-start.3
  119.6 16.5 %collective-permute-start = (bf16[1024,256]{1,0:T(8,128)(2,1)S(1)}, bf16[1024,256]{1,0:T(8,128)(2,1)S(1)}, u32[]{:S(2)}, u32[]{:S(2)}) collective-permute-start(bf16[1024,256]{1,0:T(8,128)(2,1)S(1)} %get-tuple-element.308), channel_id=1, source_target_pairs={{8,0},{16,8},{24,16},{32,24},{40,32},{48,40},{56,48},{64,56},{72,6... | collective-permute-start | bytes 1572872 | tf_op jit(solution)/shard_map/while/body/eval_jaxpr/ppermute | solution.py:11
  137.6 16.7 %collective-permute-start = (bf16[1024,256]{1,0:T(8,128)(2,1)S(1)}, bf16[1024,256]{1,0:T(8,128)(2,1)S(1)}, u32[]{:S(2)}, u32[]{:S(2)}) collective-permute-start(bf16[1024,256]{1,0:T(8,128)(2,1)S(1)} %get-tuple-element.308), channel_id=1, source_target_pairs={{8,0},{16,8},{24,16},{32,24},{40,32},{48,40},{56,48},{64,56},{72,6... | collective-permute-start | bytes 1572872 | tf_op jit(solution)/shard_map/while/body/eval_jaxpr/ppermute | solution.py:11
  155.7 11.4 %collective-permute-start = (bf16[1024,256]{1,0:T(8,128)(2,1)S(1)}, bf16[1024,256]{1,0:T(8,128)(2,1)S(1)}, u32[]{:S(2)}, u32[]{:S(2)}) collective-permute-start(bf16[1024,256]{1,0:T(8,128)(2,1)S(1)} %get-tuple-element.308), channel_id=1, source_target_pairs={{8,0},{16,8},{24,16},{32,24},{40,32},{48,40},{56,48},{64,56},{72,6... | collective-permute-start | bytes 1572872 | tf_op jit(solution)/shard_map/while/body/eval_jaxpr/ppermute | solution.py:11
  168.6 12.7 %collective-permute-start = (bf16[1024,256]{1,0:T(8,128)(2,1)S(1)}, bf16[1024,256]{1,0:T(8,128)(2,1)S(1)}, u32[]{:S(2)}, u32[]{:S(2)}) collective-permute-start(bf16[1024,256]{1,0:T(8,128)(2,1)S(1)} %get-tuple-element.308), channel_id=1, source_target_pairs={{8,0},{16,8},{24,16},{32,24},{40,32},{48,40},{56,48},{64,56},{72,6... | collective-permute-start | bytes 1572872 | tf_op jit(solution)/shard_map/while/body/eval_jaxpr/ppermute | solution.py:11
  182.8 15.8 %collective-permute-start = (bf16[1024,256]{1,0:T(8,128)(2,1)S(1)}, bf16[1024,256]{1,0:T(8,128)(2,1)S(1)}, u32[]{:S(2)}, u32[]{:S(2)}) collective-permute-start(bf16[1024,256]{1,0:T(8,128)(2,1)S(1)} %get-tuple-element.308), channel_id=1, source_target_pairs={{8,0},{16,8},{24,16},{32,24},{40,32},{48,40},{56,48},{64,56},{72,6... | collective-permute-start | bytes 1572872 | tf_op jit(solution)/shard_map/while/body/eval_jaxpr/ppermute | solution.py:11
  200.1 12.6 %collective-permute-start = (bf16[1024,256]{1,0:T(8,128)(2,1)S(1)}, bf16[1024,256]{1,0:T(8,128)(2,1)S(1)}, u32[]{:S(2)}, u32[]{:S(2)}) collective-permute-start(bf16[1024,256]{1,0:T(8,128)(2,1)S(1)} %get-tuple-element.308), channel_id=1, source_target_pairs={{8,0},{16,8},{24,16},{32,24},{40,32},{48,40},{56,48},{64,56},{72,6... | collective-permute-start | bytes 1572872 | tf_op jit(solution)/shard_map/while/body/eval_jaxpr/ppermute | solution.py:11
  214.1 12.6 %collective-permute-start = (bf16[1024,256]{1,0:T(8,128)(2,1)S(1)}, bf16[1024,256]{1,0:T(8,128)(2,1)S(1)}, u32[]{:S(2)}, u32[]{:S(2)}) collective-permute-start(bf16[1024,256]{1,0:T(8,128)(2,1)S(1)} %get-tuple-element.308), channel_id=1, source_target_pairs={{8,0},{16,8},{24,16},{32,24},{40,32},{48,40},{56,48},{64,56},{72,6... | collective-permute-start | bytes 1572872 | tf_op jit(solution)/shard_map/while/body/eval_jaxpr/ppermute | solution.py:11
  229.5 121.5 %copy-start.2 = (bf16[128,256]{1,0:T(8,128)(2,1)S(1)}, bf16[128,256]{1,0:T(8,128)(2,1)}, u32[]{:S(2)}) copy-start(bf16[128,256]{1,0:T(8,128)(2,1)} %param.11) | copy-start | bytes 196612
  229.5 519.5 %all-reduce.6.cloned.1.call-start = ((), (), s32[]{:S(2)}) async-start(), calls=%async_computation.1 | async-start | bytes 524288 | tf_op jit(solution)/shard_map/psum | solution.py:75
  352.9 500.5 %all-reduce.8.cloned.1.call-start = ((), (), s32[]{:S(2)}) async-start(), calls=%async_computation.2 | async-start | bytes 524288 | tf_op jit(solution)/shard_map/psum | solution.py:75
Sparse Core Ops, SparseCore 0:
  229.6 121.2 all-reduce.3
  354.4 394.5 all-reduce.5
  752.2 101.1 all-reduce.7
